TPU v7x, 32 devices: a whole 2x2x4 slice. The times are simulated.
32 devices in a mesh: row: 4 (over z), col: 8 (over y, x, core).
Axes of the slice: x: 2, y: 2, z: 4, core: 2. Of those that a mesh axis runs over, the one named last changes fastest.
Arguments:
- a_vals: bfloat16 [4, 8, 4, 8, 128, 128], P('row', 'col'), may hold values from -0.5 to 0.5
- a_rows: int32 [4, 8, 4, 8], P('row', 'col'), may hold values from 0 to 15
- a_cols: int32 [4, 8, 4, 8], P('row', 'col'), may hold values from 0 to 1
- a_live: int32 [4, 8, 4], P('row', 'col'), may hold values from 1 to 8, as said below
- p_vals: bfloat16 [64, 3, 128, 128], P(('row', 'col')), may hold values from -1 to 1
- p_cols: int32 [64, 3], replicated, may hold values from 0 to 15, as said below
Outputs:
- coarse_op: float32 [16, 16, 128, 128], P('col', 'row')
Inputs may be any that keep to these rules, and one draw needn't show every extreme that they name: Only slots t < a_live[r, c, s] carry blocks of A; the values in the other slots are not part of A. In every draw some grid position has all its sections full. `p_cols`: the 3 coarse block columns of a fine block row i are distinct and lie in the 4 coarse blocks from (i // 16) * 4 on.
All inputs are finite; a program needn't handle non-finite values.
Results may differ from a plain program's by a relative error of at most 0.0029.
Values may be sent and summed in bfloat16 or wider, within the bound.
No kernel may reach another device: no remote copies, remote signals or barrier semaphores. Data moves between devices by JAX's collectives and lax.ppermute only.
A program may use at most 128 MiB of HBM per device.

v0:
```python
import jax
import jax.numpy as jnp
from jax import lax
from jax.sharding import PartitionSpec as P

CROW = 4


def local(a_vals, a_rows, a_cols, a_live, p_vals, p_cols):
    row_count = lax.axis_size("row")
    col_count = lax.axis_size("col")
    grid_row = lax.axis_index("row")
    grid_col = lax.axis_index("col")
    segment = p_vals.shape[0]
    per_row = p_vals.shape[1]
    block_size = p_vals.shape[2]
    slot_count = a_vals.shape[3]
    section_vals = a_vals.reshape(row_count, slot_count, block_size, block_size)
    section_rows = a_rows.reshape(row_count, slot_count)
    section_cols = a_cols.reshape(row_count, slot_count)
    section_live = a_live.reshape(row_count)
    fine_span = segment * col_count
    coarse_total = CROW * row_count
    left_all = lax.all_gather(p_vals, "col", axis=0, tiled=True)
    left_coarse = (
        lax.dynamic_slice_in_dim(p_cols, grid_row * fine_span, fine_span, 0) - grid_row * CROW
    )
    right_coarse = lax.dynamic_index_in_dim(
        p_cols.reshape(row_count, col_count, segment, per_row), grid_col, 1, keepdims=False
    ).reshape(row_count * segment, per_row)
    initial = jnp.zeros((coarse_total, CROW, block_size, block_size), jnp.float32)
    row_labels = lax.iota(jnp.int32, CROW)
    col_labels = lax.iota(jnp.int32, coarse_total)

    def add_slots(partial_value, values, fine_rows, source_index, usable, source, source_coarse):
        right_blocks = jnp.take(source, source_index, axis=0)
        products = jnp.einsum(
            "sij,spjk->spik", values, right_blocks, preferred_element_type=jnp.float32
        )
        products = jnp.where(usable[:, None, None, None], products, 0.0).astype(jnp.bfloat16)
        left_blocks = jnp.take(left_all, fine_rows, axis=0)
        coarse_row = jnp.take(left_coarse, fine_rows, axis=0)
        row_pick = (coarse_row[:, :, None] == row_labels[None, None, :]).astype(jnp.bfloat16)
        folded = jnp.einsum(
            "saq,saji->sqji", row_pick, left_blocks, preferred_element_type=jnp.float32
        ).astype(jnp.bfloat16)
        triple = jnp.einsum(
            "sqji,spjk->spqik", folded, products, preferred_element_type=jnp.float32
        )
        coarse_col = jnp.take(source_coarse, source_index, axis=0)
        col_pick = (coarse_col[:, :, None] == col_labels[None, None, :]).astype(jnp.float32)
        flat_terms = triple.reshape(-1, CROW * block_size * block_size)
        flat_pick = col_pick.reshape(-1, coarse_total)
        added = jnp.einsum("sj,sx->jx", flat_pick, flat_terms, precision=lax.Precision.HIGHEST)
        return partial_value + added.reshape(coarse_total, CROW, block_size, block_size)

    def add_section(partial_value, section_at, source, source_coarse, source_start, piece_len):
        values = lax.dynamic_index_in_dim(section_vals, section_at, 0, keepdims=False)
        fine_rows = lax.dynamic_index_in_dim(section_rows, section_at, 0, keepdims=False)
        fine_cols = lax.dynamic_index_in_dim(section_cols, section_at, 0, keepdims=False)
        live_count = lax.dynamic_index_in_dim(section_live, section_at, 0, keepdims=False)
        target = section_at * segment + fine_cols
        inside = (target >= source_start) & (target < source_start + piece_len)
        source_index = jnp.clip(target - source_start, 0, piece_len - 1)
        position = lax.iota(jnp.int32, slot_count)
        usable = inside & (position < live_count)
        return add_slots(
            partial_value, values, fine_rows, source_index, usable, source, source_coarse
        )

    right_all = lax.all_gather(p_vals, "row", axis=0, tiled=True)

    def whole_section(section_at, running):
        return add_section(running, section_at, right_all, right_coarse, 0, row_count * segment)

    partial_value = lax.fori_loop(0, row_count, whole_section, initial)
    return lax.psum_scatter(partial_value, "col", scatter_dimension=0, tiled=True)


def solution(mesh):
    return jax.shard_map(
        local,
        mesh=mesh,
        in_specs=(
            P("row", "col", None, None, None, None),
            P("row", "col", None, None),
            P("row", "col", None, None),
            P("row", "col", None),
            P(("row", "col"), None, None, None),
            P(),
        ),
        out_specs=P("col", "row", None, None),
        check_vma=False,
    )
```

profile of v0, /device:TPU:0, one launch (start us, length us, event | category | flops | bytes accessed | tf_op | source)
XLA Modules:
  0.0 262.2 jit_solution(9492211815750386809)
XLA Ops:
  9.1 21.5 %all_gather.6 = bf16[8,3,128,128]{3,2,1,0:T(8,128)(2,1)S(1)} all-gather(bf16[2,3,128,128]{3,2,1,0:T(8,128)(2,1)} %param.12), channel_id=1, replica_groups=mesh['row'=4,'col'=8] {'row'}, dimensions={0}, use_global_device_ids=true | all-gather | bytes 983040 | tf_op jit(solution)/shard_map/all_gather | solution.py:71
  30.6 7.1 %all-gather.2.cloned.1.call-done = bf16[16,3,128,128]{3,2,1,0:T(8,128)(2,1)} async-done(((bf16[2,3,128,128]{3,2,1,0:T(8,128)(2,1)}), bf16[16,3,128,128]{3,2,1,0:T(8,128)(2,1)}) %all-gather.2.cloned.1.call-update) | async-done | bytes 1572880 | tf_op jit(solution)/shard_map/all_gather | solution.py:24
  37.7 160.7 %while.14 = (s32[]{:T(128)}, f32[16,4,128,128]{3,0,2,1:T(8,128)}, s32[4,8]{1,0:T(4,128)}, s32[8,3]{1,0:T(8,128)S(1)}, s32[4]{0:T(128)}, /*index=5*/bf16[8,3,128,...) while((s32[]{:T(128)}, f32[16,4,128,128]{3,0,2,1:T(8,128)}, ...), condition=%wide.region_1.2_spmd.clone, body=%wide.region_0.1_spmd.clone.sunk | while | flops 812649216 | bytes 100935528 | solution.py:76
  46.0 5.0 %convolution_bitcast_fusion.2 = f32[8,3,4,128,128]{3,4,2,1,0:T(8,128)} fusion(bf16[8,4,128,128,1]{3,1,2,0,4:T(4,128)(2,1)S(1)} %fusion.57, bf16[8,3,128,128]{3,2,1,0:T(8,128)(2,1)S(1)} %gather_fusion.2, pred[8]{0:T(512)(128)(4,1)S(1)} %compare_and_fusion.3, pred[8]{0:T(512)(128)(4,1)S(1)} %get-tuple-element.331, ...), kind=kOutput, calls=%fused_computation.9.clone.1 | convolution fusion | flops 504496128 | bytes 8388628 | tf_op jit(solution)/shard_map/while/body/eval_jaxpr/sqji,spjk->spqik/dot_general | solution.py:47
  51.0 6.6 %copy.49 = f32[8,3,4,128,128]{4,3,2,1,0:T(8,128)} copy(f32[8,3,4,128,128]{3,4,2,1,0:T(8,128)} %convolution_bitcast_fusion.2) | data formatting | bytes 12582912 | tf_op jit(solution)/shard_map/while/body/eval_jaxpr/sqji,spjk->spqik/transpose | solution.py:47
  57.6 6.8 %reshape.248 = f32[24,65536]{1,0:T(8,128)} reshape(f32[8,3,4,128,128]{4,3,2,1,0:T(8,128)} %copy.49) | data formatting | bytes 12582912 | tf_op jit(solution)/shard_map/while/body/eval_jaxpr/reshape | solution.py:52
  64.4 4.0 %copy.50 = f32[3,8,512,128]{3,2,1,0:T(8,128)S(1)} copy(f32[3,8,512,128]{3,1,2,0:T(8,128)} %bitcast.89) | data formatting | bytes 12582912 | tf_op jit(solution)/shard_map/while
  68.4 7.4 %select_add_fusion.2 = f32[16,4,128,128]{3,0,2,1:T(8,128)S(1)} fusion(f32[16,4,128,128]{3,0,2,1:T(8,128)S(1)} %copy-done, f32[4,128,128,24]{2,1,0,3:T(8,128)S(1)} %bitcast.90, pred[]{:T(512)S(6)} %compare.3, s32[24]{0:T(128)S(1)} %select_n.169), kind=kOutput, calls=%fused_computation.8.clone.1 | convolution fusion | flops 304087424 | bytes 14680161 | tf_op jit(solution)/shard_map/while/body/eval_jaxpr/sj,sx->jx/dot_general | solution.py:54
  86.2 5.0 %convolution_bitcast_fusion.2 = f32[8,3,4,128,128]{3,4,2,1,0:T(8,128)} fusion(bf16[8,4,128,128,1]{3,1,2,0,4:T(4,128)(2,1)S(1)} %fusion.57, bf16[8,3,128,128]{3,2,1,0:T(8,128)(2,1)S(1)} %gather_fusion.2, pred[8]{0:T(512)(128)(4,1)S(1)} %compare_and_fusion.3, pred[8]{0:T(512)(128)(4,1)S(1)} %get-tuple-element.331, ...), kind=kOutput, calls=%fused_computation.9.clone.1 | convolution fusion | flops 504496128 | bytes 8388628 | tf_op jit(solution)/shard_map/while/body/eval_jaxpr/sqji,spjk->spqik/dot_general | solution.py:47
  91.2 6.6 %copy.49 = f32[8,3,4,128,128]{4,3,2,1,0:T(8,128)} copy(f32[8,3,4,128,128]{3,4,2,1,0:T(8,128)} %convolution_bitcast_fusion.2) | data formatting | bytes 12582912 | tf_op jit(solution)/shard_map/while/body/eval_jaxpr/sqji,spjk->spqik/transpose | solution.py:47
  97.7 6.8 %reshape.248 = f32[24,65536]{1,0:T(8,128)} reshape(f32[8,3,4,128,128]{4,3,2,1,0:T(8,128)} %copy.49) | data formatting | bytes 12582912 | tf_op jit(solution)/shard_map/while/body/eval_jaxpr/reshape | solution.py:52
  104.6 4.0 %copy.50 = f32[3,8,512,128]{3,2,1,0:T(8,128)S(1)} copy(f32[3,8,512,128]{3,1,2,0:T(8,128)} %bitcast.89) | data formatting | bytes 12582912 | tf_op jit(solution)/shard_map/while
  108.6 7.4 %select_add_fusion.2 = f32[16,4,128,128]{3,0,2,1:T(8,128)S(1)} fusion(f32[16,4,128,128]{3,0,2,1:T(8,128)S(1)} %copy-done, f32[4,128,128,24]{2,1,0,3:T(8,128)S(1)} %bitcast.90, pred[]{:T(512)S(6)} %compare.3, s32[24]{0:T(128)S(1)} %select_n.169), kind=kOutput, calls=%fused_computation.8.clone.1 | convolution fusion | flops 304087424 | bytes 14680161 | tf_op jit(solution)/shard_map/while/body/eval_jaxpr/sj,sx->jx/dot_general | solution.py:54
  126.4 5.0 %convolution_bitcast_fusion.2 = f32[8,3,4,128,128]{3,4,2,1,0:T(8,128)} fusion(bf16[8,4,128,128,1]{3,1,2,0,4:T(4,128)(2,1)S(1)} %fusion.57, bf16[8,3,128,128]{3,2,1,0:T(8,128)(2,1)S(1)} %gather_fusion.2, pred[8]{0:T(512)(128)(4,1)S(1)} %compare_and_fusion.3, pred[8]{0:T(512)(128)(4,1)S(1)} %get-tuple-element.331, ...), kind=kOutput, calls=%fused_computation.9.clone.1 | convolution fusion | flops 504496128 | bytes 8388628 | tf_op jit(solution)/shard_map/while/body/eval_jaxpr/sqji,spjk->spqik/dot_general | solution.py:47
  131.3 6.6 %copy.49 = f32[8,3,4,128,128]{4,3,2,1,0:T(8,128)} copy(f32[8,3,4,128,128]{3,4,2,1,0:T(8,128)} %convolution_bitcast_fusion.2) | data formatting | bytes 12582912 | tf_op jit(solution)/shard_map/while/body/eval_jaxpr/sqji,spjk->spqik/transpose | solution.py:47
  137.9 6.8 %reshape.248 = f32[24,65536]{1,0:T(8,128)} reshape(f32[8,3,4,128,128]{4,3,2,1,0:T(8,128)} %copy.49) | data formatting | bytes 12582912 | tf_op jit(solution)/shard_map/while/body/eval_jaxpr/reshape | solution.py:52
  144.8 4.0 %copy.50 = f32[3,8,512,128]{3,2,1,0:T(8,128)S(1)} copy(f32[3,8,512,128]{3,1,2,0:T(8,128)} %bitcast.89) | data formatting | bytes 12582912 | tf_op jit(solution)/shard_map/while
  148.8 7.4 %select_add_fusion.2 = f32[16,4,128,128]{3,0,2,1:T(8,128)S(1)} fusion(f32[16,4,128,128]{3,0,2,1:T(8,128)S(1)} %copy-done, f32[4,128,128,24]{2,1,0,3:T(8,128)S(1)} %bitcast.90, pred[]{:T(512)S(6)} %compare.3, s32[24]{0:T(128)S(1)} %select_n.169), kind=kOutput, calls=%fused_computation.8.clone.1 | convolution fusion | flops 304087424 | bytes 14680161 | tf_op jit(solution)/shard_map/while/body/eval_jaxpr/sj,sx->jx/dot_general | solution.py:54
  166.5 5.0 %convolution_bitcast_fusion.2 = f32[8,3,4,128,128]{3,4,2,1,0:T(8,128)} fusion(bf16[8,4,128,128,1]{3,1,2,0,4:T(4,128)(2,1)S(1)} %fusion.57, bf16[8,3,128,128]{3,2,1,0:T(8,128)(2,1)S(1)} %gather_fusion.2, pred[8]{0:T(512)(128)(4,1)S(1)} %compare_and_fusion.3, pred[8]{0:T(512)(128)(4,1)S(1)} %get-tuple-element.331, ...), kind=kOutput, calls=%fused_computation.9.clone.1 | convolution fusion | flops 504496128 | bytes 8388628 | tf_op jit(solution)/shard_map/while/body/eval_jaxpr/sqji,spjk->spqik/dot_general | solution.py:47
  171.5 6.6 %copy.49 = f32[8,3,4,128,128]{4,3,2,1,0:T(8,128)} copy(f32[8,3,4,128,128]{3,4,2,1,0:T(8,128)} %convolution_bitcast_fusion.2) | data formatting | bytes 12582912 | tf_op jit(solution)/shard_map/while/body/eval_jaxpr/sqji,spjk->spqik/transpose | solution.py:47
  178.1 6.8 %reshape.248 = f32[24,65536]{1,0:T(8,128)} reshape(f32[8,3,4,128,128]{4,3,2,1,0:T(8,128)} %copy.49) | data formatting | bytes 12582912 | tf_op jit(solution)/shard_map/while/body/eval_jaxpr/reshape | solution.py:52
  189.0 7.4 %select_add_fusion.2 = f32[16,4,128,128]{3,0,2,1:T(8,128)S(1)} fusion(f32[16,4,128,128]{3,0,2,1:T(8,128)S(1)} %copy-done, f32[4,128,128,24]{2,1,0,3:T(8,128)S(1)} %bitcast.90, pred[]{:T(512)S(6)} %compare.3, s32[24]{0:T(128)S(1)} %select_n.169), kind=kOutput, calls=%fused_computation.8.clone.1 | convolution fusion | flops 304087424 | bytes 14680161 | tf_op jit(solution)/shard_map/while/body/eval_jaxpr/sj,sx->jx/dot_general | solution.py:54
  198.3 5.5 %copy.22 = f32[16,4,128,128]{3,2,1,0:T(8,128)} copy(f32[16,4,128,128]{3,0,2,1:T(8,128)} %get-tuple-element.204) | data formatting | bytes 8388608 | tf_op jit(solution)/shard_map/while | solution.py:76
  203.9 51.5 %reduce-scatter.2.cloned.1.call-done = f32[2,4,128,128]{3,2,1,0:T(8,128)} async-done(((f32[16,4,128,128]{3,2,1,0:T(8,128)}), f32[2,4,128,128]{3,2,1,0:T(8,128)}) %reduce-scatter.2.cloned.1.call-update) | async-done | bytes 524304 | tf_op jit(solution)/shard_map/reduce_scatter | solution.py:77
  (92 shorter events, 47.4 us)
Async XLA Ops:
  6.5 31.1 %all-gather.2.cloned.1.call-start = ((), (), s32[]{:S(2)}) async-start(), calls=%async_computation.1 | async-start | bytes 1769472 | tf_op jit(solution)/shard_map/all_gather | solution.py:24
  7.3 248.1 %reduce-scatter.2.cloned.1.call-start = ((), (), s32[]{:S(2)}) async-start(), calls=%async_computation.2 | async-start | bytes 4718592 | tf_op jit(solution)/shard_map/reduce_scatter | solution.py:77
  64.4 4.0 %copy-start = (f32[16,4,128,128]{3,0,2,1:T(8,128)S(1)}, f32[16,4,128,128]{3,0,2,1:T(8,128)}, u32[]{:S(2)}) copy-start(f32[16,4,128,128]{3,0,2,1:T(8,128)} %get-tuple-element.346) | copy-start | bytes 12582916 | tf_op jit(solution)/shard_map/while
  75.9 1.9 copy-start.1
  104.6 4.0 %copy-start = (f32[16,4,128,128]{3,0,2,1:T(8,128)S(1)}, f32[16,4,128,128]{3,0,2,1:T(8,128)}, u32[]{:S(2)}) copy-start(f32[16,4,128,128]{3,0,2,1:T(8,128)} %get-tuple-element.346) | copy-start | bytes 12582916 | tf_op jit(solution)/shard_map/while
  116.1 1.9 copy-start.1
  144.8 4.0 %copy-start = (f32[16,4,128,128]{3,0,2,1:T(8,128)S(1)}, f32[16,4,128,128]{3,0,2,1:T(8,128)}, u32[]{:S(2)}) copy-start(f32[16,4,128,128]{3,0,2,1:T(8,128)} %get-tuple-element.346) | copy-start | bytes 12582916 | tf_op jit(solution)/shard_map/while
  156.2 1.9 copy-start.1
  184.9 4.0 %copy-start = (f32[16,4,128,128]{3,0,2,1:T(8,128)S(1)}, f32[16,4,128,128]{3,0,2,1:T(8,128)}, u32[]{:S(2)}) copy-start(f32[16,4,128,128]{3,0,2,1:T(8,128)} %get-tuple-element.346) | copy-start | bytes 12582916 | tf_op jit(solution)/shard_map/while
  196.4 1.9 copy-start.1
Sparse Core Ops, SparseCore 0:
  9.2 28.3 all-gather.1
  204.0 51.3 reduce-scatter.1
where the time goes:
time: 263 us; the launch traced here: 262 us
  local copies, waits for them, and re-layouts  106 us (40%)
  waiting for transfers between devices  59.3 us (23%)
  matrix products  52.8 us (20%)
  blocking collectives  21.5 us (8%)
  between operations  13.4 us (5%)
  other arithmetic  9.08 us (3%)
    reduce_scatter x1, waiting for transfers between devices, local(): lax.psum_scatter(partial_value, 'col', scatter_dimension=0, tiled=True)  51.5 us
    dot_general x4, matrix products, add_slots(): jnp.einsum('sj,sx->jx', flat_pick, flat_terms, precision=lax.Precision.HI...  29.8 us
    reshape x4, local copies, waits for them, and re-layouts, add_slots(): flat_terms = triple.reshape(-1, CROW * block_size * block_size)  27.4 us
    transpose x4, local copies, waits for them, and re-layouts, add_slots(): jnp.einsum('sqji,spjk->spqik', folded, products, preferred_element_type=j...  26.3 us
    while x20, local copies, waits for them, and re-layouts  23.8 us
    all_gather x1, blocking collectives, local(): right_all = lax.all_gather(p_vals, 'row', axis=0, tiled=True)  21.5 us
    dot_general x4, matrix products, add_slots(): jnp.einsum('sqji,spjk->spqik', folded, products, preferred_element_type=j...  19.9 us
    gather x4, local copies, waits for them, and re-layouts, add_slots(): left_blocks = jnp.take(left_all, fine_rows, axis=0)  8.43 us
  transfers between devices with their start and end apart: 2, of which 2 were waited for; matrix products, arithmetic and copies ran while one was open for 1% of the time, Pallas kernels for 0%

commit v1 on v0

--- a/solution.py
+++ b/solution.py
@@ -4,6 +4,19 @@
 from jax.sharding import PartitionSpec as P
 
 CROW = 4
+
+
+def gather_around(array, axis, dim):
+    peers, index, rows = (lax.axis_size(axis), lax.axis_index(axis), array.shape[dim])
+    right = [(i, (i + 1) % peers) for i in range(peers)]
+    whole = jnp.zeros((*array.shape[:dim], peers * rows, *array.shape[dim + 1 :]), array.dtype)
+    held = array
+    for step in range(peers):
+        owner = (index - step) % peers
+        whole = lax.dynamic_update_slice_in_dim(whole, held, owner * rows, axis=dim)
+        if step < peers - 1:
+            held = lax.ppermute(held, axis, right)
+    return whole
 
 
 def local(a_vals, a_rows, a_cols, a_live, p_vals, p_cols):
@@ -68,7 +81,7 @@
             partial_value, values, fine_rows, source_index, usable, source, source_coarse
         )
 
-    right_all = lax.all_gather(p_vals, "row", axis=0, tiled=True)
+    right_all = gather_around(p_vals, "row", 0)
 
     def whole_section(section_at, running):
         return add_section(running, section_at, right_all, right_coarse, 0, row_count * segment)

time: 263 us -> 264 us (level)
  blocking collectives: 21.5 us -> 0 us
  waiting for transfers between devices: 59.3 us -> 76.5 us
  starting transfers between devices: 0.04 us -> 3.12 us
    all_gather x1 -> x0, blocking collectives: 21.5 us -> none  [local(): right_all = lax.all_gather(p_vals, 'row', axis=0, tiled=True)]
    ppermute x0 -> x3, waiting for transfers between devices: none -> 19.5 us  [gather_around(): held = lax.ppermute(held, axis, right)]
    ppermute x0 -> x3, starting transfers between devices: none -> 3.08 us  [gather_around(): held = lax.ppermute(held, axis, right)]
  transfers between devices with their start and end apart: 2 -> 5, of which waited for: 2 -> 5; matrix products, arithmetic and copies ran while one was open for 1% -> 1% of each run, Pallas kernels for 0% -> 0%
where the time goes in v1:
time: 264 us; the launch traced here: 263 us
  local copies, waits for them, and re-layouts  107 us (41%)
  waiting for transfers between devices  76.5 us (29%)
  matrix products  52.9 us (20%)
  between operations  13.4 us (5%)
  other arithmetic  9.38 us (4%)
  starting transfers between devices  3.12 us (1%)
    reduce_scatter x1, waiting for transfers between devices, local(): lax.psum_scatter(partial_value, 'col', scatter_dimension=0, tiled=True)  51.4 us
    dot_general x4, matrix products, add_slots(): jnp.einsum('sj,sx->jx', flat_pick, flat_terms, precision=lax.Precision.HI...  29.8 us
    reshape x4, local copies, waits for them, and re-layouts, add_slots(): flat_terms = triple.reshape(-1, CROW * block_size * block_size)  27.4 us
    transpose x4, local copies, waits for them, and re-layouts, add_slots(): jnp.einsum('sqji,spjk->spqik', folded, products, preferred_element_type=j...  26.3 us
    while x20, local copies, waits for them, and re-layouts  23.8 us
    dot_general x4, matrix products, add_slots(): jnp.einsum('sqji,spjk->spqik', folded, products, preferred_element_type=j...  20 us
    ppermute x3, waiting for transfers between devices, gather_around(): held = lax.ppermute(held, axis, right)  19.5 us
    gather x4, local copies, waits for them, and re-layouts, add_slots(): left_blocks = jnp.take(left_all, fine_rows, axis=0)  8.43 us
  transfers between devices with their start and end apart: 5, of which 5 were waited for; matrix products, arithmetic and copies ran while one was open for 1% of the time, Pallas kernels for 0%

profile of v1, /device:TPU:0, one launch (start us, length us, event | category | flops | bytes accessed | tf_op | source)
XLA Modules:
  0.0 262.7 jit_solution(5231867114966661604)
XLA Ops:
  13.3 4.2 %collective-permute-done = bf16[2,3,128,128]{3,2,1,0:T(8,128)(2,1)S(1)} collective-permute-done((bf16[2,3,128,128]{3,2,1,0:T(8,128)(2,1)}, bf16[2,3,128,128]{3,2,1,0:T(8,128)(2,1)S(1)}, u32[]{:S(2)}, u32[]{:S(2)}) %collective-permute-start) | collective-permute-done | bytes 196640 | tf_op jit(solution)/shard_map/ppermute | solution.py:18
  17.5 7.9 %collective-permute-done.1 = bf16[2,3,128,128]{3,2,1,0:T(8,128)(2,1)S(1)} collective-permute-done((bf16[2,3,128,128]{3,2,1,0:T(8,128)(2,1)S(1)}, bf16[2,3,128,128]{3,2,1,0:T(8,128)(2,1)S(1)}, u32[]{:S(2)}, u32[]{:S(2)}) %collective-permute-start.1) | collective-permute-done | bytes 196640 | tf_op jit(solution)/shard_map/ppermute | solution.py:18
  25.5 7.4 %collective-permute-done.2 = bf16[2,3,128,128]{3,2,1,0:T(8,128)(2,1)S(1)} collective-permute-done((bf16[2,3,128,128]{3,2,1,0:T(8,128)(2,1)S(1)}, bf16[2,3,128,128]{3,2,1,0:T(8,128)(2,1)S(1)}, u32[]{:S(2)}, u32[]{:S(2)}) %collective-permute-start.2) | collective-permute-done | bytes 196640 | tf_op jit(solution)/shard_map/ppermute | solution.py:18
  32.9 4.8 %all-gather.2.cloned.1.call-done = bf16[16,3,128,128]{3,2,1,0:T(8,128)(2,1)} async-done(((bf16[2,3,128,128]{3,2,1,0:T(8,128)(2,1)}), bf16[16,3,128,128]{3,2,1,0:T(8,128)(2,1)}) %all-gather.2.cloned.1.call-update) | async-done | bytes 1572880 | tf_op jit(solution)/shard_map/all_gather | solution.py:37
  37.7 161.2 %while.14 = (s32[]{:T(128)}, f32[16,4,128,128]{3,0,2,1:T(8,128)}, s32[4,8]{1,0:T(4,128)}, s32[8,3]{1,0:T(8,128)S(1)}, s32[4]{0:T(128)}, /*index=5*/bf16[8,3,128,...) while((s32[]{:T(128)}, f32[16,4,128,128]{3,0,2,1:T(8,128)}, ...), condition=%wide.region_1.2_spmd.clone, body=%wide.region_0.1_spmd.clone.sunk | while | flops 812649216 | bytes 100935528 | solution.py:89
  46.1 5.0 %convolution_bitcast_fusion.2 = f32[8,3,4,128,128]{3,4,2,1,0:T(8,128)} fusion(bf16[8,4,128,128,1]{3,1,2,0,4:T(4,128)(2,1)S(1)} %fusion.57, bf16[8,3,128,128]{3,2,1,0:T(8,128)(2,1)S(1)} %gather_fusion.2, pred[8]{0:T(512)(128)(4,1)S(1)} %compare_and_fusion.3, pred[8]{0:T(512)(128)(4,1)S(1)} %get-tuple-element.331, ...), kind=kOutput, calls=%fused_computation.9.clone.1 | convolution fusion | flops 504496128 | bytes 8388628 | tf_op jit(solution)/shard_map/while/body/eval_jaxpr/sqji,spjk->spqik/dot_general | solution.py:60
  51.1 6.6 %copy.49 = f32[8,3,4,128,128]{4,3,2,1,0:T(8,128)} copy(f32[8,3,4,128,128]{3,4,2,1,0:T(8,128)} %convolution_bitcast_fusion.2) | data formatting | bytes 12582912 | tf_op jit(solution)/shard_map/while/body/eval_jaxpr/sqji,spjk->spqik/transpose | solution.py:60
  57.7 6.9 %reshape.248 = f32[24,65536]{1,0:T(8,128)} reshape(f32[8,3,4,128,128]{4,3,2,1,0:T(8,128)} %copy.49) | data formatting | bytes 12582912 | tf_op jit(solution)/shard_map/while/body/eval_jaxpr/reshape | solution.py:65
  64.6 4.0 %copy.50 = f32[3,8,512,128]{3,2,1,0:T(8,128)S(1)} copy(f32[3,8,512,128]{3,1,2,0:T(8,128)} %bitcast.89) | data formatting | bytes 12582912 | tf_op jit(solution)/shard_map/while
  68.6 7.4 %select_add_fusion.2 = f32[16,4,128,128]{3,0,2,1:T(8,128)S(1)} fusion(f32[16,4,128,128]{3,0,2,1:T(8,128)S(1)} %copy-done, f32[4,128,128,24]{2,1,0,3:T(8,128)S(1)} %bitcast.90, pred[]{:T(512)S(6)} %compare.7, s32[24]{0:T(128)S(1)} %select_n.208), kind=kOutput, calls=%fused_computation.8.clone.1 | convolution fusion | flops 304087424 | bytes 14680161 | tf_op jit(solution)/shard_map/while/body/eval_jaxpr/sj,sx->jx/dot_general | solution.py:67
  86.4 5.0 %convolution_bitcast_fusion.2 = f32[8,3,4,128,128]{3,4,2,1,0:T(8,128)} fusion(bf16[8,4,128,128,1]{3,1,2,0,4:T(4,128)(2,1)S(1)} %fusion.57, bf16[8,3,128,128]{3,2,1,0:T(8,128)(2,1)S(1)} %gather_fusion.2, pred[8]{0:T(512)(128)(4,1)S(1)} %compare_and_fusion.3, pred[8]{0:T(512)(128)(4,1)S(1)} %get-tuple-element.331, ...), kind=kOutput, calls=%fused_computation.9.clone.1 | convolution fusion | flops 504496128 | bytes 8388628 | tf_op jit(solution)/shard_map/while/body/eval_jaxpr/sqji,spjk->spqik/dot_general | solution.py:60
  91.4 6.6 %copy.49 = f32[8,3,4,128,128]{4,3,2,1,0:T(8,128)} copy(f32[8,3,4,128,128]{3,4,2,1,0:T(8,128)} %convolution_bitcast_fusion.2) | data formatting | bytes 12582912 | tf_op jit(solution)/shard_map/while/body/eval_jaxpr/sqji,spjk->spqik/transpose | solution.py:60
  98.0 6.9 %reshape.248 = f32[24,65536]{1,0:T(8,128)} reshape(f32[8,3,4,128,128]{4,3,2,1,0:T(8,128)} %copy.49) | data formatting | bytes 12582912 | tf_op jit(solution)/shard_map/while/body/eval_jaxpr/reshape | solution.py:65
  108.9 7.4 %select_add_fusion.2 = f32[16,4,128,128]{3,0,2,1:T(8,128)S(1)} fusion(f32[16,4,128,128]{3,0,2,1:T(8,128)S(1)} %copy-done, f32[4,128,128,24]{2,1,0,3:T(8,128)S(1)} %bitcast.90, pred[]{:T(512)S(6)} %compare.7, s32[24]{0:T(128)S(1)} %select_n.208), kind=kOutput, calls=%fused_computation.8.clone.1 | convolution fusion | flops 304087424 | bytes 14680161 | tf_op jit(solution)/shard_map/while/body/eval_jaxpr/sj,sx->jx/dot_general | solution.py:67
  126.7 5.0 %convolution_bitcast_fusion.2 = f32[8,3,4,128,128]{3,4,2,1,0:T(8,128)} fusion(bf16[8,4,128,128,1]{3,1,2,0,4:T(4,128)(2,1)S(1)} %fusion.57, bf16[8,3,128,128]{3,2,1,0:T(8,128)(2,1)S(1)} %gather_fusion.2, pred[8]{0:T(512)(128)(4,1)S(1)} %compare_and_fusion.3, pred[8]{0:T(512)(128)(4,1)S(1)} %get-tuple-element.331, ...), kind=kOutput, calls=%fused_computation.9.clone.1 | convolution fusion | flops 504496128 | bytes 8388628 | tf_op jit(solution)/shard_map/while/body/eval_jaxpr/sqji,spjk->spqik/dot_general | solution.py:60
  131.7 6.6 %copy.49 = f32[8,3,4,128,128]{4,3,2,1,0:T(8,128)} copy(f32[8,3,4,128,128]{3,4,2,1,0:T(8,128)} %convolution_bitcast_fusion.2) | data formatting | bytes 12582912 | tf_op jit(solution)/shard_map/while/body/eval_jaxpr/sqji,spjk->spqik/transpose | solution.py:60
  138.3 6.9 %reshape.248 = f32[24,65536]{1,0:T(8,128)} reshape(f32[8,3,4,128,128]{4,3,2,1,0:T(8,128)} %copy.49) | data formatting | bytes 12582912 | tf_op jit(solution)/shard_map/while/body/eval_jaxpr/reshape | solution.py:65
  149.2 7.4 %select_add_fusion.2 = f32[16,4,128,128]{3,0,2,1:T(8,128)S(1)} fusion(f32[16,4,128,128]{3,0,2,1:T(8,128)S(1)} %copy-done, f32[4,128,128,24]{2,1,0,3:T(8,128)S(1)} %bitcast.90, pred[]{:T(512)S(6)} %compare.7, s32[24]{0:T(128)S(1)} %select_n.208), kind=kOutput, calls=%fused_computation.8.clone.1 | convolution fusion | flops 304087424 | bytes 14680161 | tf_op jit(solution)/shard_map/while/body/eval_jaxpr/sj,sx->jx/dot_general | solution.py:67
  167.0 5.0 %convolution_bitcast_fusion.2 = f32[8,3,4,128,128]{3,4,2,1,0:T(8,128)} fusion(bf16[8,4,128,128,1]{3,1,2,0,4:T(4,128)(2,1)S(1)} %fusion.57, bf16[8,3,128,128]{3,2,1,0:T(8,128)(2,1)S(1)} %gather_fusion.2, pred[8]{0:T(512)(128)(4,1)S(1)} %compare_and_fusion.3, pred[8]{0:T(512)(128)(4,1)S(1)} %get-tuple-element.331, ...), kind=kOutput, calls=%fused_computation.9.clone.1 | convolution fusion | flops 504496128 | bytes 8388628 | tf_op jit(solution)/shard_map/while/body/eval_jaxpr/sqji,spjk->spqik/dot_general | solution.py:60
  172.0 6.6 %copy.49 = f32[8,3,4,128,128]{4,3,2,1,0:T(8,128)} copy(f32[8,3,4,128,128]{3,4,2,1,0:T(8,128)} %convolution_bitcast_fusion.2) | data formatting | bytes 12582912 | tf_op jit(solution)/shard_map/while/body/eval_jaxpr/sqji,spjk->spqik/transpose | solution.py:60
  178.6 6.9 %reshape.248 = f32[24,65536]{1,0:T(8,128)} reshape(f32[8,3,4,128,128]{4,3,2,1,0:T(8,128)} %copy.49) | data formatting | bytes 12582912 | tf_op jit(solution)/shard_map/while/body/eval_jaxpr/reshape | solution.py:65
  189.5 7.4 %select_add_fusion.2 = f32[16,4,128,128]{3,0,2,1:T(8,128)S(1)} fusion(f32[16,4,128,128]{3,0,2,1:T(8,128)S(1)} %copy-done, f32[4,128,128,24]{2,1,0,3:T(8,128)S(1)} %bitcast.90, pred[]{:T(512)S(6)} %compare.7, s32[24]{0:T(128)S(1)} %select_n.208), kind=kOutput, calls=%fused_computation.8.clone.1 | convolution fusion | flops 304087424 | bytes 14680161 | tf_op jit(solution)/shard_map/while/body/eval_jaxpr/sj,sx->jx/dot_general | solution.py:67
  198.9 5.5 %copy.22 = f32[16,4,128,128]{3,2,1,0:T(8,128)} copy(f32[16,4,128,128]{3,0,2,1:T(8,128)} %get-tuple-element.204) | data formatting | bytes 8388608 | tf_op jit(solution)/shard_map/while | solution.py:89
  204.4 51.4 %reduce-scatter.2.cloned.1.call-done = f32[2,4,128,128]{3,2,1,0:T(8,128)} async-done(((f32[16,4,128,128]{3,2,1,0:T(8,128)}), f32[2,4,128,128]{3,2,1,0:T(8,128)}) %reduce-scatter.2.cloned.1.call-update) | async-done | bytes 524304 | tf_op jit(solution)/shard_map/reduce_scatter | solution.py:90
  (102 shorter events, 60.1 us)
Async XLA Ops:
  6.5 31.1 %all-gather.2.cloned.1.call-start = ((), (), s32[]{:S(2)}) async-start(), calls=%async_computation.1 | async-start | bytes 1769472 | tf_op jit(solution)/shard_map/all_gather | solution.py:37
  7.3 248.6 %reduce-scatter.2.cloned.1.call-start = ((), (), s32[]{:S(2)}) async-start(), calls=%async_computation.2 | async-start | bytes 4718592 | tf_op jit(solution)/shard_map/reduce_scatter | solution.py:90
  7.3 10.2 %collective-permute-start = (bf16[2,3,128,128]{3,2,1,0:T(8,128)(2,1)}, bf16[2,3,128,128]{3,2,1,0:T(8,128)(2,1)S(1)}, u32[]{:S(2)}, u32[]{:S(2)}) collective-permute-start(bf16[2,3,128,128]{3,2,1,0:T(8,128)(2,1)} %param.12), channel_id=1, source_target_pairs={{0,8},{8,16},{16,24},{24,0},{1,9},{9,17},{17,25},{25,1},{2,10},{10... | collective-permute-start | bytes 589832 | tf_op jit(solution)/shard_map/ppermute | solution.py:18
  17.5 7.9 %collective-permute-start.1 = (bf16[2,3,128,128]{3,2,1,0:T(8,128)(2,1)S(1)}, bf16[2,3,128,128]{3,2,1,0:T(8,128)(2,1)S(1)}, u32[]{:S(2)}, u32[]{:S(2)}) collective-permute-start(bf16[2,3,128,128]{3,2,1,0:T(8,128)(2,1)S(1)} %collective-permute-done), channel_id=1, source_target_pairs={{0,8},{8,16},{16,24},{24,0},{1,9},{9,17},{17,25},{25,1},{2,10},{10... | collective-permute-start | bytes 589832 | tf_op jit(solution)/shard_map/ppermute | solution.py:18
  25.4 7.5 %collective-permute-start.2 = (bf16[2,3,128,128]{3,2,1,0:T(8,128)(2,1)S(1)}, bf16[2,3,128,128]{3,2,1,0:T(8,128)(2,1)S(1)}, u32[]{:S(2)}, u32[]{:S(2)}) collective-permute-start(bf16[2,3,128,128]{3,2,1,0:T(8,128)(2,1)S(1)} %collective-permute-done.1), channel_id=1, source_target_pairs={{0,8},{8,16},{16,24},{24,0},{1,9},{9,17},{17,25},{25,1},{2,10},{10... | collective-permute-start | bytes 589832 | tf_op jit(solution)/shard_map/ppermute | solution.py:18
  64.6 4.0 %copy-start = (f32[16,4,128,128]{3,0,2,1:T(8,128)S(1)}, f32[16,4,128,128]{3,0,2,1:T(8,128)}, u32[]{:S(2)}) copy-start(f32[16,4,128,128]{3,0,2,1:T(8,128)} %get-tuple-element.346) | copy-start | bytes 12582916 | tf_op jit(solution)/shard_map/while
  76.0 1.9 copy-start.1
  104.9 4.0 %copy-start = (f32[16,4,128,128]{3,0,2,1:T(8,128)S(1)}, f32[16,4,128,128]{3,0,2,1:T(8,128)}, u32[]{:S(2)}) copy-start(f32[16,4,128,128]{3,0,2,1:T(8,128)} %get-tuple-element.346) | copy-start | bytes 12582916 | tf_op jit(solution)/shard_map/while
  116.3 1.9 copy-start.1
  145.2 4.0 %copy-start = (f32[16,4,128,128]{3,0,2,1:T(8,128)S(1)}, f32[16,4,128,128]{3,0,2,1:T(8,128)}, u32[]{:S(2)}) copy-start(f32[16,4,128,128]{3,0,2,1:T(8,128)} %get-tuple-element.346) | copy-start | bytes 12582916 | tf_op jit(solution)/shard_map/while
  156.6 1.9 copy-start.1
  185.5 4.0 %copy-start = (f32[16,4,128,128]{3,0,2,1:T(8,128)S(1)}, f32[16,4,128,128]{3,0,2,1:T(8,128)}, u32[]{:S(2)}) copy-start(f32[16,4,128,128]{3,0,2,1:T(8,128)} %get-tuple-element.346) | copy-start | bytes 12582916 | tf_op jit(solution)/shard_map/while
  196.9 1.9 copy-start.1
Sparse Core Ops, SparseCore 0:
  9.2 28.3 all-gather.1
  204.5 51.2 reduce-scatter.1
